TPU v7x, 128 devices: a whole 4x4x4 slice. The times are simulated.
128 devices in a mesh: row: 8 (over x, z_lo), col: 16 (over z_hi, y, core).
Axes of the slice: x: 4, y: 4, z: 4 (z_hi: 2, z_lo: 2; z = z_hi * 2 + z_lo), core: 2. Of those that a mesh axis runs over, the one named last changes fastest.
Arguments:
- pixels: bfloat16 [64, 64000, 144], P(None, ('row', 'col')), may hold values from 0.049804688 to 4
- match_filter: bfloat16 [64000, 2, 144], P(('row', 'col')), may hold values from -48 to 48
- tile_ranks: int32 [64, 256], P('row', 'col'), may hold values from 1 to 64
- column_order: int32 [256], replicated, may hold values from 0 to 255, each once
- right_factors: bfloat16 [64, 256, 64, 500], P('row', 'col'), may hold values from -0.25 to 0.25
- left_factors: bfloat16 [64, 256, 64, 500], P('row', 'col'), may hold values from -0.046875 to 0.046875
Outputs:
- commands: float32 [64, 32000], P(None, ('row', 'col'))
Inputs may be any that keep to these rules, and one draw needn't show every extreme that they name: `column_order`: every slope block is read by exactly one tile column.
All inputs are finite; a program needn't handle non-finite values.
Results may differ from a plain program's by a relative error of at most 0.0041.
Values may be sent and summed in bfloat16 or wider, within the bound.
A program may use at most 128 MiB of HBM per device.

v0:
```python
import jax
import jax.numpy as jnp
from jax import lax
from jax.sharding import PartitionSpec as P


def in_blocks(value, dim, size):
    dims = value.shape
    parts = value.reshape(*dims[:dim], size, dims[dim] // size, *dims[dim + 1 :])
    return jnp.moveaxis(parts, dim, 0)


def summed_on_arrival(value, axis, dim):
    parts = in_blocks(value, dim, lax.axis_size(axis))
    arrived = lax.all_to_all(parts, axis, split_axis=0, concat_axis=0, tiled=True)
    return arrived.sum(axis=0)


def centroid(frame_pixels, match_filter):
    flux = jnp.sum(frame_pixels.astype(jnp.float32), axis=2)
    raw = jnp.einsum("fsp,skp->fsk", frame_pixels, match_filter, preferred_element_type=jnp.float32)
    slopes = (raw / flux[:, :, None]).astype(jnp.bfloat16)
    return slopes.reshape(frame_pixels.shape[0], -1)


def route(slopes, order_mine, inverse, tile_width, col_count):
    frame_count = slopes.shape[0]
    block_count = slopes.shape[1] // tile_width
    own_blocks = jnp.transpose(slopes.reshape(frame_count, block_count, tile_width), (1, 0, 2))
    row_index = lax.axis_index("row")
    col_index = lax.axis_index("col")
    device_rank = row_index * col_count + col_index
    block_ids = device_rank * block_count + jnp.arange(block_count, dtype=jnp.int32)
    column_span = order_mine.shape[0]
    target = jnp.take(inverse, block_ids) // column_span
    selector = (jnp.arange(col_count, dtype=jnp.int32)[:, None] == target[None, :]).astype(
        jnp.bfloat16
    )
    outgoing = selector[:, :, None, None] * own_blocks[None]
    received = lax.all_to_all(outgoing, "col", split_axis=0, concat_axis=0, tiled=True)
    source_cols = jnp.arange(col_count, dtype=jnp.int32)
    source_ids = (
        (row_index * col_count + source_cols)[:, None] * block_count
        + jnp.arange(block_count, dtype=jnp.int32)[None, :]
    ).reshape(-1)
    tile_column = jnp.take(inverse, source_ids)
    valid = tile_column // column_span == col_index
    local_slot = tile_column - col_index * column_span
    placement = (
        (jnp.arange(column_span, dtype=jnp.int32)[:, None] == local_slot[None, :]) & valid[None, :]
    ).astype(jnp.bfloat16)
    flat_blocks = received.reshape(col_count * block_count, frame_count * tile_width)
    placed = jnp.dot(placement, flat_blocks, preferred_element_type=jnp.float32)
    summed = lax.psum(placed.astype(jnp.bfloat16), "row")
    return summed.reshape(column_span, frame_count, tile_width)


def shards(pixels, match_filter, tile_ranks, column_order, right_factors, left_factors):
    frame_count = pixels.shape[0]
    tile_width = right_factors.shape[3]
    rank_bound = right_factors.shape[2]
    column_span = right_factors.shape[1]
    col_count = lax.axis_size("col")
    col_index = lax.axis_index("col")
    order_mine = lax.dynamic_slice_in_dim(column_order, col_index * column_span, column_span)
    inverse = jnp.argsort(column_order, stable=True)
    slopes = centroid(pixels, match_filter)
    pieces = route(slopes, order_mine, inverse, tile_width, col_count)
    projection = jnp.einsum(
        "ijkt,jft->ijkf", right_factors, pieces, preferred_element_type=jnp.float32
    )
    component = lax.broadcasted_iota(jnp.int32, (1, 1, rank_bound), 2)
    keep = component < tile_ranks[:, :, None]
    projection = jnp.where(keep[:, :, :, None], projection, 0.0).astype(jnp.bfloat16)
    partial_cmd = jnp.einsum(
        "ijkf,ijka->fia", projection, left_factors, preferred_element_type=jnp.float32
    )
    partial_cmd = partial_cmd.reshape(frame_count, -1)
    return summed_on_arrival(partial_cmd, "col", 1)


def solution(mesh):
    in_specs = (
        P(None, ("row", "col"), None),
        P(("row", "col"), None, None),
        P("row", "col"),
        P(),
        P("row", "col", None, None),
        P("row", "col", None, None),
    )
    out_specs = P(None, ("row", "col"))
    return jax.shard_map(shards, mesh=mesh, in_specs=in_specs, out_specs=out_specs, check_vma=False)
```

profile of v0, /device:TPU:1, one launch (start us, length us, event | category | flops | bytes accessed | tf_op | source)
XLA Modules:
  0.0 222.4 jit_solution(16440297610372381009)
XLA Ops:
  6.5 24.2 %copy.15 = bf16[64,500,144]{2,0,1:T(8,128)(2,1)} copy(bf16[64,500,144]{1,2,0:T(8,128)(2,1)} %param.6) | data formatting | bytes 18432000 | tf_op args[0]
  30.8 0.0 copy-start.2
  30.8 0.0 copy-start
  30.8 6.0 %convert_reduce_fusion = f32[64,500]{1,0:T(8,128)S(1)} fusion(bf16[64,500,144]{1,2,0:T(8,128)(2,1)} %param.6), kind=kLoop, calls=%fused_computation.3 | loop fusion | flops 9184000 | bytes 9344000 | tf_op jit(solution)/shard_map/reduce_sum | solution.py:20
  36.8 0.0 copy-done.2
  36.9 3.2 %sort.17 = (s32[256]{0:T(256)}, s32[256]{0:T(256)S(1)}) sort(s32[256]{0:T(256)S(1)} %copy-done.2, s32[256]{0:T(256)S(1)} %iota.38), dimensions={0}, to_apply=%region_0.0 | sort | flops 2048 | bytes 4096 | tf_op jit(solution)/shard_map/jit(argsort)/sort | solution.py:66
  40.0 0.6 gather_fusion.1
  40.7 0.0 copy-done
  40.7 0.9 copy.14
  41.6 0.1 copy.16
  41.7 10.0 %fusion.2 = bf16[64,500,2]{0,2,1:T(2,128)(2,1)S(1)} fusion(bf16[500,2,144]{2,1,0:T(2,128)(2,1)S(1)} %copy.14, bf16[64,500,144]{2,0,1:T(8,128)(2,1)} %copy.15, f32[64,500]{0,1:T(8,128)S(1)} %copy.16), kind=kOutput, calls=%fused_computation.9 | convolution fusion | flops 18560000 | bytes 9760000 | tf_op jit(solution)/shard_map/fsp,skp->fsk/dot_general | solution.py:21
  51.7 0.1 reshape_reshape.6
  51.8 0.2 copy.17
  52.0 0.0 copy-start.1
  52.0 1.6 broadcast_multiply_fusion
  53.5 9.3 %all-to-all-start = ((bf16[16,2,64,500]{3,2,1,0:T(8,128)(2,1)}), bf16[16,2,64,500]{3,2,1,0:T(8,128)(2,1)S(1)}, u32[]{:S(2)}, u32[]{:S(2)}) async-start(bf16[16,2,64,500]{3,2,1,0:T(8,128)(2,1)} %broadcast_multiply_fusion), calls=%async_computation | async-start | bytes 4194304 | tf_op jit(solution)/shard_map/all_to_all | solution.py:40
  62.8 0.2 all-reduce.2.cloned.1.call-start
  63.1 0.1 iota_add_fusion
  63.2 0.1 add.139
  63.2 0.1 add.136
  63.4 0.7 gather_fusion
  64.1 27.3 %all-to-all-done = bf16[16,2,64,500]{3,2,1,0:T(8,128)(2,1)S(1)} async-done(((bf16[16,2,64,500]{3,2,1,0:T(8,128)(2,1)}), bf16[16,2,64,500]{3,2,1,0:T(8,128)(2,1)S(1)}, u32[]{:S(2)}, u32[]{:S(2)}) %all-to-all-start) | async-done | bytes 2048032 | tf_op jit(solution)/shard_map/all_to_all | solution.py:40
  91.4 3.5 %reshape.169 = bf16[32,32000]{1,0:T(8,128)(2,1)} reshape(bf16[16,2,64,500]{3,2,1,0:T(8,128)(2,1)S(1)} %all-to-all-done) | data formatting | bytes 4096000 | tf_op jit(solution)/shard_map/reshape | solution.py:52
  94.9 2.0 convolution_convert_fusion
  96.9 3.4 %reshape.170 = bf16[16,64,500]{2,1,0:T(8,128)(2,1)} reshape(bf16[16,32000]{1,0:T(8,128)(2,1)S(1)} %convolution_convert_fusion) | data formatting | bytes 2048000 | tf_op jit(solution)/shard_map/reshape | solution.py:55
  100.3 0.0 all-reduce.2.cloned.1.call-update
  100.3 0.0 copy-done.1
  100.4 0.1 iota_compare_fusion
  100.4 73.1 %all-reduce.2.cloned.1.call-done = bf16[16,64,500]{2,1,0:T(8,128)(2,1)} async-done(((bf16[16,64,500]{2,1,0:T(8,128)(2,1)}), bf16[16,64,500]{2,1,0:T(8,128)(2,1)}) %all-reduce.2.cloned.1.call-update) | async-done | bytes 1024016 | tf_op jit(solution)/shard_map/psum | solution.py:54
  173.5 11.6 %convolution_bitcast_fusion = f32[64,8,500]{2,0,1:T(8,128)S(1)} fusion(bf16[8,16,64,500]{3,2,1,0:T(8,128)(2,1)} %param.11, bf16[8,16,64,500]{3,2,1,0:T(8,128)(2,1)} %param.10, pred[8,16,64]{2,1,0:T(8,128)(4,1)S(1)} %iota_compare_fusion, bf16[16,64,500]{2,1,0:T(8,128)(2,1)} %all-reduce.2.cloned.1.call-done), kind=kOutput, calls=%fused_computation.6 | convolution fusion | flops 1049624576 | bytes 18440192 | tf_op jit(solution)/shard_map/ijkf,ijka->fia/dot_general | solution.py:75
  185.2 0.6 copy.18
  185.8 0.3 reshape_reshape.7
  186.1 0.6 copy.19
  186.7 28.2 %all_to_all.10 = f32[16,64,250]{2,1,0:T(8,128)S(1)} all-to-all(f32[16,64,250]{2,1,0:T(8,128)S(1)} %copy.19), channel_id=1, replica_groups=mesh['row'=8,'col'=16] {'col'}, dimensions={0} | all-to-all | bytes 2048000 | tf_op jit(solution)/shard_map/all_to_all | solution.py:15
  214.9 0.7 reduce_sum.19
  (10 shorter events, 0.1 us)
Async XLA Ops:
  30.8 6.1 %copy-start.2 = (s32[256]{0:T(256)S(1)}, s32[256]{0:T(256)}, u32[]{:S(2)}) copy-start(s32[256]{0:T(256)} %param.9) | copy-start | bytes 3076
  30.8 9.9 %copy-start = (bf16[500,2,144]{0,2,1:T(8,128)(2,1)S(1)}, bf16[500,2,144]{0,2,1:T(8,128)(2,1)}, u32[]{:S(2)}) copy-start(bf16[500,2,144]{0,2,1:T(8,128)(2,1)} %param.7) | copy-start | bytes 864004
  52.0 48.4 %copy-start.1 = (s32[8,16]{1,0:T(8,128)S(1)}, s32[8,16]{1,0:T(8,128)}, u32[]{:S(2)}) copy-start(s32[8,16]{1,0:T(8,128)} %param.8) | copy-start | bytes 1540
  53.5 37.9 %all-to-all-start = ((bf16[16,2,64,500]{3,2,1,0:T(8,128)(2,1)}), bf16[16,2,64,500]{3,2,1,0:T(8,128)(2,1)S(1)}, u32[]{:S(2)}, u32[]{:S(2)}) async-start(bf16[16,2,64,500]{3,2,1,0:T(8,128)(2,1)} %broadcast_multiply_fusion), calls=%async_computation | async-start | bytes 4194304 | tf_op jit(solution)/shard_map/all_to_all | solution.py:40
  62.8 110.7 %all-reduce.2.cloned.1.call-start = ((), (), s32[]{:S(2)}) async-start(), calls=%async_computation.2 | async-start | bytes 2097152 | tf_op jit(solution)/shard_map/psum | solution.py:54
Sparse Core Ops, SparseCore 0:
  100.5 73.0 all-reduce.1
where the time goes:
time: 223 us; the launch traced here: 222 us
  waiting for transfers between devices  100 us (45%)
  local copies, waits for them, and re-layouts  35.4 us (16%)
  blocking collectives  28.2 us (13%)
  matrix products  23.6 us (11%)
  between operations  13.6 us (6%)
  other arithmetic  11.7 us (5%)
  starting transfers between devices  9.52 us (4%)
    psum x1, waiting for transfers between devices, route(): summed = lax.psum(placed.astype(jnp.bfloat16), 'row')  73.1 us
    all_to_all x1, blocking collectives, summed_on_arrival(): lax.all_to_all(parts, axis, split_axis=0, concat_axis=0, tiled=True)  28.2 us
    all_to_all x1, waiting for transfers between devices, route(): lax.all_to_all(outgoing, 'col', split_axis=0, concat_axis=0, tiled=True)  27.3 us
    unnamed x8, local copies, waits for them, and re-layouts  25.1 us
    dot_general x1, matrix products, shards(): jnp.einsum('ijkf,ijka->fia', projection, left_factors, preferred_element_...  11.6 us
    dot_general x1, matrix products, centroid(): jnp.einsum('fsp,skp->fsk', frame_pixels, match_filter, preferred_element_...  10 us
    all_to_all x1, starting transfers between devices, route(): lax.all_to_all(outgoing, 'col', split_axis=0, concat_axis=0, tiled=True)  9.3 us
    reduce_sum x1, other arithmetic, centroid(): flux = jnp.sum(frame_pixels.astype(jnp.float32), axis=2)  6.03 us
  transfers between devices with their start and end apart: 2, of which 2 were waited for; matrix products, arithmetic and copies ran while one was open for 0% of the time, Pallas kernels for 0%

commit v1 on v0

v1 whole, which is shorter than its diff:
```python
import jax
import jax.numpy as jnp
from jax import lax
from jax.experimental import pallas as pl
from jax.experimental.pallas import tpu as pltpu
from jax.sharding import PartitionSpec as P

BF16 = jnp.bfloat16
F32 = jnp.float32
ROWS, COLS = 8, 16
FRAMES, SUBS, PIX = 64, 500, 144
TILE, RANK = 500, 64
SPAN_I, SPAN_J = 8, 16
HALF = 250
PIX_CHUNKS = 8
CHUNK_FRAMES = FRAMES // PIX_CHUNKS
R_CHUNKS = 4
R_COLS = SPAN_J // R_CHUNKS
GATHER_CHUNKS = 4
PAIRS = SPAN_J // 2
CHUNK_PAIRS = PAIRS // GATHER_CHUNKS


def one_hot(shape, target_of_row):
    row = lax.broadcasted_iota(jnp.int32, shape, 0)
    col = lax.broadcasted_iota(jnp.int32, shape, 1)
    return jnp.where(col == target_of_row(row), 1.0, 0.0).astype(BF16)


def permute(matrix, rows):
    return jnp.dot(matrix, rows, preferred_element_type=F32).astype(BF16)


def kernel(
    order_ref, ranks_ref, pix_hbm, filt_hbm, right_hbm, left_hbm, out_ref,
    pix, filt, filt32, right, left, slopes, sel, by_row, from_row, by_mid, at_mid, by_col, from_col,
    mine_u, gathered, proj, other_half, my_half, half_in, chunk_out, chunk_in,
    filt_sem, pix_sem, right_sem, left_sem,
    a1_send, a1_recv, a2_send, a2_recv, a3_send, a3_recv, b_send, b_recv,
    c1_send, c1_recv, c2_send, c2_recv,
):
    r = lax.axis_index("row")
    c = lax.axis_index("col")
    group = c // 2
    core = c % 2

    def row_peer(d):
        return lax.rem(r + d, ROWS)

    def col_peer(d):
        return lax.rem(c + d, COLS)

    def pix_copy(n):
        frames = pl.ds(n * CHUNK_FRAMES, CHUNK_FRAMES)
        return pltpu.make_async_copy(pix_hbm.at[frames], pix.at[frames], pix_sem.at[n])

    def right_copy(n):
        cols = pl.ds(n * R_COLS, R_COLS)
        return pltpu.make_async_copy(right_hbm.at[:, cols], right.at[:, cols], right_sem.at[n])

    def left_copy(n):
        return pltpu.make_async_copy(left_hbm.at[n], left.at[n], left_sem.at[n])

    filt_copy = pltpu.make_async_copy(filt_hbm, filt, filt_sem)
    filt_copy.start()
    for n in range(PIX_CHUNKS):
        pix_copy(n).start()
    for n in range(R_CHUNKS):
        right_copy(n).start()
    for n in range(SPAN_I):
        left_copy(n).start()

    barrier = pltpu.get_barrier_semaphore()
    for d in range(1, ROWS):
        pl.semaphore_signal(barrier, inc=1, device_id={"row": row_peer(d)}, device_id_type=pl.DeviceIdType.MESH)
    for d in range(1, COLS):
        pl.semaphore_signal(barrier, inc=1, device_id={"col": col_peer(d)}, device_id_type=pl.DeviceIdType.MESH)

    row_z = lax.broadcasted_iota(jnp.int32, (256, 256), 0)
    block_of_row = ((row_z >> 1) & 7) * 32 + (row_z >> 4) * 2 + (row_z & 1)
    sel[...] = jnp.where(block_of_row == order_ref[...], 1.0, 0.0).T.astype(BF16)
    slopes[...] = jnp.zeros_like(slopes)

    filt_copy.wait()
    filt32[...] = filt[...].astype(F32)

    def centroid(n, carry):
        pix_copy(n).wait()
        for lane in range(4):
            low, high = lane * 128, min(lane * 128 + 128, SUBS)
            width = high - low

            def add(p, sums):
                rows = pl.ds(pl.multiple_of(p * 16, 16), 16)
                fx = filt32[0, rows, low:high]
                fy = filt32[1, rows, low:high]
                new = []
                for f in range(CHUNK_FRAMES):
                    v = pix[n * CHUNK_FRAMES + f, rows, low:high].astype(F32)
                    vx, vy = v * fx, v * fy
                    s, sx, sy = sums[3 * f : 3 * f + 3]
                    new += [s + (v[:8] + v[8:]), sx + (vx[:8] + vx[8:]), sy + (vy[:8] + vy[8:])]
                return tuple(new)

            zero = jnp.zeros((8, width), F32)
            sums = lax.fori_loop(0, PIX // 16, add, (zero,) * (3 * CHUNK_FRAMES))

            def total(kind):
                return jnp.concatenate(
                    [jnp.sum(sums[3 * f + kind], axis=0, keepdims=True) for f in range(CHUNK_FRAMES)], axis=0
                )

            flux = total(0)
            frames = pl.ds(pl.multiple_of(n * CHUNK_FRAMES, 8), CHUNK_FRAMES)
            slopes[0, frames, low:high] = total(1) / flux
            slopes[1, frames, low:high] = total(2) / flux
        return carry

    lax.fori_loop(0, PIX_CHUNKS, centroid, 0)

    parts = []
    for b in range(2):
        kinds = [slopes[k] if b == 0 else pltpu.roll(slopes[k], 512 - HALF, 1) for k in range(2)]
        for h in range(2):
            parts.append(jnp.concatenate([v[:, h * 128 : h * 128 + 128] for v in kinds], axis=1))
    raw = jnp.concatenate(parts, axis=0).astype(BF16)
    lanes = one_hot((256, 256), lambda row: (row & 127) * 2 + (row >> 7))
    order_rows = one_hot(
        (256, 256), lambda row: (row & 1) * 128 + ((row >> 4) & 1) * 64 + (row >> 5) * 8 + ((row >> 1) & 7)
    )
    by_row[...] = permute(order_rows, permute(raw, lanes)).reshape(ROWS, 32, 256)

    pl.semaphore_wait(barrier, ROWS - 1 + COLS - 1)

    def remote(src, dst, send, recv, device):
        return pltpu.make_async_remote_copy(
            src_ref=src, dst_ref=dst, send_sem=send, recv_sem=recv,
            device_id=device, device_id_type=pl.DeviceIdType.MESH,
        )

    a1 = [
        remote(by_row.at[row_peer(d)], from_row.at[r], a1_send.at[d - 1], a1_recv.at[d - 1], {"row": row_peer(d)})
        for d in range(1, ROWS)
    ]
    for copy in a1:
        copy.start()
    from_row[r] = by_row[r]
    middle = one_hot((256, 256), lambda row: ((row >> 1) & 7) * 32 + (row >> 4) * 2 + (row & 1))
    for copy in a1:
        copy.wait_recv()
    by_mid[...] = permute(middle, from_row[...].reshape(256, 256)).reshape(COLS, 16, 256)

    a2 = [
        remote(by_mid.at[col_peer(d)], at_mid.at[c], a2_send.at[d - 1], a2_recv.at[d - 1], {"col": col_peer(d)})
        for d in range(1, COLS)
    ]
    for copy in a2:
        copy.start()
    at_mid[c] = by_mid[c]
    for copy in a2:
        copy.wait_recv()
    by_col[...] = permute(sel[...], at_mid[...].reshape(256, 256)).reshape(COLS, 16, 256)

    a3 = [
        remote(by_col.at[col_peer(d)], from_col.at[c], a3_send.at[d - 1], a3_recv.at[d - 1], {"col": col_peer(d)})
        for d in range(1, COLS)
    ]
    for copy in a3:
        copy.start()
    from_col[c] = by_col[c]
    frame_rows = one_hot((128, 128), lambda row: (row & 7) * 16 + (row >> 3))
    for copy in a3:
        copy.wait_recv()
    for h in range(2):
        piece = from_col[h * 8 : h * 8 + 8].reshape(128, 256)
        mine_u[:, :, h * 256 : h * 256 + 256] = permute(frame_rows, piece).reshape(PAIRS, 16, 256)

    def gather_copy(n, d):
        pairs = pl.ds(n * CHUNK_PAIRS, CHUNK_PAIRS)
        return remote(
            mine_u.at[pairs], gathered.at[r, pairs], b_send.at[n, d - 1], b_recv.at[n, d - 1], {"row": row_peer(d)}
        )

    for n in range(GATHER_CHUNKS):
        for d in range(1, ROWS):
            gather_copy(n, d).start()
    gathered[r] = mine_u[...]

    lane_id = lax.broadcasted_iota(jnp.int32, (FRAMES, 128), 1)
    low_half = lane_id < RANK
    component = lane_id & (RANK - 1)

    def project(n, carry):
        right_copy(n).wait()
        for d in range(1, ROWS):
            gather_copy(n, d).wait_recv()
        for q in range(CHUNK_PAIRS):
            pair = n * CHUNK_PAIRS + q
            both = gathered[:, pair].astype(F32)
            halves = []
            for e in range(2):
                piece = both[:, e * 8 : e * 8 + 8, :].reshape(FRAMES, 512).astype(BF16)
                factors = right[:, 2 * pair + e].reshape(SPAN_I * RANK, TILE)
                halves.append(
                    lax.dot_general(
                        piece[:, :TILE], factors, (((1,), (1,)), ((), ())), preferred_element_type=F32
                    )
                )
            for i2 in range(SPAN_I // 2):
                kept = []
                for e in range(2):
                    bound = jnp.where(
                        low_half, ranks_ref[2 * i2, 2 * pair + e], ranks_ref[2 * i2 + 1, 2 * pair + e]
                    )
                    kept.append(jnp.where(component < bound, halves[e][:, i2 * 128 : i2 * 128 + 128], 0.0))
                proj[2 * i2, pair] = jnp.where(low_half, kept[0], pltpu.roll(kept[1], RANK, 1)).astype(BF16)
                proj[2 * i2 + 1, pair] = jnp.where(low_half, pltpu.roll(kept[0], RANK, 1), kept[1]).astype(BF16)
        return carry

    lax.fori_loop(0, GATHER_CHUNKS, project, 0)

    for n in range(SPAN_I):
        left_copy(n).wait()

    def half_copy(s):
        return remote(
            other_half.at[s], half_in.at[s], c1_send.at[s], c1_recv.at[s], {"col": c + 1 - 2 * core}
        )

    def tile_of(s):
        return lax.rem(group + 1 + s, SPAN_I)

    def chunk_copy(s):
        return remote(
            chunk_out.at[s], chunk_in.at[s], c2_send.at[s], c2_recv.at[s], {"col": 2 * tile_of(s) + core}
        )

    def finish(s):
        half_copy(s).wait_recv()
        chunk_out[s] = (my_half[s] + half_in[s]).astype(BF16)
        chunk_copy(s).start()

    def command(s, carry):
        i = tile_of(s)
        lhs = jnp.concatenate([proj[i, q] for q in range(PAIRS)], axis=1)
        full = jnp.dot(lhs, left[i].reshape(SPAN_J * RANK, TILE), preferred_element_type=F32)
        lower, upper = full[:, :HALF], full[:, HALF:]
        first = core == 0
        my_half[s] = jnp.where(first, lower, upper)
        other_half[s] = jnp.where(first, upper, lower)
        half_copy(s).start()

        @pl.when(s >= 1)
        def _():
            finish(s - 1)

        return carry

    lax.fori_loop(0, SPAN_I, command, 0)
    last = SPAN_I - 1
    half_copy(last).wait_recv()
    total_cmd = my_half[last] + half_in[last]
    for s in range(last):
        chunk_copy(s).wait_recv()
        total_cmd += chunk_in[s].astype(F32)
    out_ref[...] = total_cmd

    for copy in a1 + a2 + a3:
        copy.wait_send()
    for n in range(GATHER_CHUNKS):
        for d in range(1, ROWS):
            gather_copy(n, d).wait_send()
    for s in range(SPAN_I):
        half_copy(s).wait_send()
    for s in range(last):
        chunk_copy(s).wait_send()


def shards(pixels, match_filter, tile_ranks, column_order, right_factors, left_factors):
    hbm = pl.BlockSpec(memory_space=pl.ANY)
    dma = pltpu.SemaphoreType.DMA
    return pl.pallas_call(
        kernel,
        out_shape=jax.ShapeDtypeStruct((FRAMES, HALF), F32),
        in_specs=[
            pl.BlockSpec(memory_space=pltpu.VMEM),
            pl.BlockSpec(memory_space=pltpu.SMEM),
            hbm, hbm, hbm, hbm,
        ],
        out_specs=pl.BlockSpec(memory_space=pltpu.VMEM),
        scratch_shapes=[
            pltpu.VMEM((FRAMES, PIX, SUBS), BF16),
            pltpu.VMEM((2, PIX, SUBS), BF16),
            pltpu.VMEM((2, PIX, SUBS), F32),
            pltpu.VMEM((SPAN_I, SPAN_J, RANK, TILE), BF16),
            pltpu.VMEM((SPAN_I, SPAN_J, RANK, TILE), BF16),
            pltpu.VMEM((2, FRAMES, 512), F32),
            pltpu.VMEM((256, 256), BF16),
            pltpu.VMEM((ROWS, 32, 256), BF16),
            pltpu.VMEM((ROWS, 32, 256), BF16),
            pltpu.VMEM((COLS, 16, 256), BF16),
            pltpu.VMEM((COLS, 16, 256), BF16),
            pltpu.VMEM((COLS, 16, 256), BF16),
            pltpu.VMEM((COLS, 16, 256), BF16),
            pltpu.VMEM((PAIRS, 16, 512), BF16),
            pltpu.VMEM((ROWS, PAIRS, 16, 512), BF16),
            pltpu.VMEM((SPAN_I, PAIRS, FRAMES, 128), BF16),
            pltpu.VMEM((SPAN_I, FRAMES, HALF), F32),
            pltpu.VMEM((SPAN_I, FRAMES, HALF), F32),
            pltpu.VMEM((SPAN_I, FRAMES, HALF), F32),
            pltpu.VMEM((SPAN_I - 1, FRAMES, HALF), BF16),
            pltpu.VMEM((SPAN_I - 1, FRAMES, HALF), BF16),
            dma, dma((PIX_CHUNKS,)), dma((R_CHUNKS,)), dma((SPAN_I,)),
            dma((ROWS - 1,)), dma((ROWS - 1,)),
            dma((COLS - 1,)), dma((COLS - 1,)),
            dma((COLS - 1,)), dma((COLS - 1,)),
            dma((GATHER_CHUNKS, ROWS - 1)), dma((GATHER_CHUNKS, ROWS - 1)),
            dma((SPAN_I,)), dma((SPAN_I,)),
            dma((SPAN_I - 1,)), dma((SPAN_I - 1,)),
        ],
        compiler_params=pltpu.CompilerParams(
            collective_id=0, has_side_effects=True, vmem_limit_bytes=48 * 1024 * 1024
        ),
        name="frames_to_commands",
    )(
        column_order.reshape(1, -1),
        tile_ranks,
        jnp.transpose(pixels, (0, 2, 1)),
        jnp.transpose(match_filter, (1, 2, 0)),
        right_factors,
        left_factors,
    )


def solution(mesh):
    in_specs = (
        P(None, ("row", "col"), None),
        P(("row", "col"), None, None),
        P("row", "col"),
        P(),
        P("row", "col", None, None),
        P("row", "col", None, None),
    )
    out_specs = P(None, ("row", "col"))
    return jax.shard_map(shards, mesh=mesh, in_specs=in_specs, out_specs=out_specs, check_vma=False)
```

time: 223 us -> 58 us (0.26)
  waiting for transfers between devices: 100 us -> 0 us
  Pallas kernels: 0 us -> 54.8 us
  local copies, waits for them, and re-layouts: 35.4 us -> 2.96 us
  blocking collectives: 28.2 us -> 0 us
  matrix products: 23.6 us -> 0 us
  between operations: 13.6 us -> 0.01 us
  other arithmetic: 11.7 us -> 0 us
  starting transfers between devices: 9.52 us -> 0 us
    psum x1 -> x0, waiting for transfers between devices: 73.1 us -> none  [route(): summed = lax.psum(placed.astype(jnp.bfloat16), 'row')]
    pallas_call x0 -> x1, Pallas kernels: none -> 54.8 us  [shards(): pl.pallas_call(kernel, out_shape=jax.ShapeDtypeStruct((FRAMES, HALF), F32...]
    all_to_all x1 -> x0, blocking collectives: 28.2 us -> none  [summed_on_arrival(): lax.all_to_all(parts, axis, split_axis=0, concat_axis=0, tiled=True)]
    all_to_all x1 -> x0, waiting for transfers between devices: 27.3 us -> none  [route(): lax.all_to_all(outgoing, 'col', split_axis=0, concat_axis=0, tiled=True)]
    dot_general x3 -> x0, matrix products: 23.6 us -> none  [the longest x1 11.6 us: shards(): jnp.einsum('ijkf,ijka->fia', projection, left_factors, preferred_element_...]
    unnamed x8 -> x7, local copies, waits for them, and re-layouts: 25.1 us -> 2.96 us
    all_to_all x1 -> x0, starting transfers between devices: 9.3 us -> none  [route(): lax.all_to_all(outgoing, 'col', split_axis=0, concat_axis=0, tiled=True)]
    reshape x2 -> x0, local copies, waits for them, and re-layouts: 6.88 us -> none  [the longest x1 3.51 us: route(): received.reshape(col_count * block_count, frame_count * tile_width)]
  transfers between devices with their start and end apart: 2 -> 0, of which waited for: 2 -> 0; matrix products, arithmetic and copies ran while one was open for 0% -> 0% of each run, Pallas kernels for 0% -> 0%
where the time goes in v1:
time: 58 us; the launch traced here: 57.8 us
  Pallas kernels  54.8 us (94%)
  local copies, waits for them, and re-layouts  2.96 us (5%)
    pallas_call x1, Pallas kernels, shards(): pl.pallas_call(kernel, out_shape=jax.ShapeDtypeStruct((FRAMES, HALF), F32...  54.8 us
    unnamed x7, local copies, waits for them, and re-layouts  2.96 us

profile of v1, /device:TPU:1, one launch (start us, length us, event | category | flops | bytes accessed | tf_op | source)
XLA Modules:
  0.0 57.8 jit_solution(14087519347297377068)
XLA Ops:
  0.0 0.0 copy-start
  0.0 1.0 %copy-done = bf16[500,2,144]{0,2,1:T(8,128)(2,1)S(1)} copy-done((bf16[500,2,144]{0,2,1:T(8,128)(2,1)S(1)}, bf16[500,2,144]{0,2,1:T(8,128)(2,1)}, u32[]{:S(2)}) %copy-start) | copy-done | bytes 288024
  1.0 0.0 copy-start.1
  1.0 0.7 %copy-done.1 = s32[8,16]{1,0:T(8,128)S(1)} copy-done((s32[8,16]{1,0:T(8,128)S(1)}, s32[8,16]{1,0:T(8,128)}, u32[]{:S(2)}) %copy-start.1) | copy-done | bytes 536
  1.6 0.0 copy-start.2
  1.7 0.7 %copy-done.2 = s32[256]{0:T(256)S(1)} copy-done((s32[256]{0:T(256)S(1)}, s32[256]{0:T(256)}, u32[]{:S(2)}) %copy-start.2) | copy-done | bytes 1048
  2.3 54.8 %frames_to_commands.1 = f32[64,250]{1,0:T(8,128)S(1)} custom-call(s32[1,256]{1,0:T(1,128)S(1)} %bitcast.4, s32[8,16]{1,0:T(8,128)S(1)} %copy-done.1, bf16[64,144,500]{2,1,0:T(8,128)(2,1)} %bitcast.5, bf16[2,144,500]{2,1,0:T(8,128)(2,1)S(1)} %bitcast.3, bf16[8,16,64,500]{3,2,1,0:T(8,128)(2,1)} %right_hbm.1, bf16[8,16,64,500]{3,2,1,0:T(8,128)(2,1)} %left_hbm.1), custom_call_target="tpu_custom_call" | custom-call | tf_op jit(solution)/shard_map/frames_to_commands/pallas_call | solution.py:282
  57.2 0.6 %copy.8 = f32[64,250]{1,0:T(8,128)} copy(f32[64,250]{1,0:T(8,128)S(1)} %frames_to_commands.1) | data formatting | bytes 128000
Async XLA Ops:
  0.0 1.0 %copy-start = (bf16[500,2,144]{0,2,1:T(8,128)(2,1)S(1)}, bf16[500,2,144]{0,2,1:T(8,128)(2,1)}, u32[]{:S(2)}) copy-start(bf16[500,2,144]{0,2,1:T(8,128)(2,1)} %param.7) | copy-start | bytes 864004
  1.0 0.7 %copy-start.1 = (s32[8,16]{1,0:T(8,128)S(1)}, s32[8,16]{1,0:T(8,128)}, u32[]{:S(2)}) copy-start(s32[8,16]{1,0:T(8,128)} %ranks_ref.1) | copy-start | bytes 1540
  1.6 0.7 %copy-start.2 = (s32[256]{0:T(256)S(1)}, s32[256]{0:T(256)}, u32[]{:S(2)}) copy-start(s32[256]{0:T(256)} %param.9) | copy-start | bytes 3076

commit v2 on v1

v2 whole, which is shorter than its diff:
```python
import jax
import jax.numpy as jnp
from jax import lax
from jax.experimental import pallas as pl
from jax.experimental.pallas import tpu as pltpu
from jax.sharding import PartitionSpec as P

BF16 = jnp.bfloat16
F32 = jnp.float32
ROWS, COLS = 8, 16
FRAMES, SUBS, PIX = 64, 500, 144
TILE, RANK = 500, 64
SPAN_I, SPAN_J = 8, 16
HALF = 250
PIX_CHUNKS = 8
CHUNK_FRAMES = FRAMES // PIX_CHUNKS
R_CHUNKS = 4
R_COLS = SPAN_J // R_CHUNKS
PAIRS = SPAN_J // 2
CHUNK_PAIRS = PAIRS // R_CHUNKS
DEVICES = ROWS * COLS
MESH = pl.DeviceIdType.MESH


def one_hot(shape, target_of_row):
    row = lax.broadcasted_iota(jnp.int32, shape, 0)
    col = lax.broadcasted_iota(jnp.int32, shape, 1)
    return jnp.where(col == target_of_row(row), 1.0, 0.0).astype(BF16)


def permute(matrix, rows):
    return jnp.dot(matrix, rows, preferred_element_type=F32).astype(BF16)


def kernel(
    order_hbm, ranks_hbm, pix_hbm, filt_hbm, right_hbm, left_hbm, out_ref,
    order, ranks, pix, filt, filt32, right, left, slopes, sel, lanes, frame_rows, rows32, by_piece, at_mid, by_col, gathered,
    pieces, proj, other_half, my_half, half_in, chunk_out, chunk_in,
    order_sem, ranks_sem, filt_sem, pix_sem, right_sem, left_sem,
    spread_send, spread_recv, gather_send, gather_recv,
    c1_send, c1_recv, c2_send, c2_recv,
):
    r = lax.axis_index("row")
    c = lax.axis_index("col")
    core = lax.rem(c, 2)
    y = lax.rem(c // 2, 4)
    z_hi = c // 8
    x = r // 2
    z = z_hi * 2 + lax.rem(r, 2)
    rank = r * COLS + c

    xs = [lax.rem(x + d, 4) for d in range(4)]
    ys = [lax.rem(y + d, 4) for d in range(4)]
    zs = [lax.rem(z + d, 4) for d in range(4)]
    cores = [core, 1 - core]
    offsets = [(dx, dy, dz, dk) for dx in range(4) for dy in range(4) for dz in range(4) for dk in range(2)]
    offsets.sort(key=lambda o: -sum(min(d, 4 - d) for d in o[:3]))
    peers = [
        (xs[dx] * 2 + lax.rem(zs[dz], 2), (zs[dz] // 2 * 4 + ys[dy]) * 2 + cores[dk])
        for dx, dy, dz, dk in offsets
        if (dx, dy, dz, dk) != (0, 0, 0, 0)
    ]

    def pix_copy(n):
        frames = pl.ds(n * CHUNK_FRAMES, CHUNK_FRAMES)
        return pltpu.make_async_copy(pix_hbm.at[frames], pix.at[frames], pix_sem.at[n])

    def right_copy(n):
        cols = pl.ds(n * R_COLS, R_COLS)
        return pltpu.make_async_copy(right_hbm.at[:, cols], right.at[:, cols], right_sem.at[n])

    def left_copy(n):
        return pltpu.make_async_copy(left_hbm.at[n], left.at[n], left_sem.at[n])

    order_copy = pltpu.make_async_copy(order_hbm, order, order_sem)
    ranks_copy = pltpu.make_async_copy(ranks_hbm, ranks, ranks_sem)
    filt_copy = pltpu.make_async_copy(filt_hbm, filt, filt_sem)
    filt_copy.start()
    order_copy.start()
    ranks_copy.start()
    for n in range(PIX_CHUNKS):
        pix_copy(n).start()
    barrier = pltpu.get_barrier_semaphore()
    for row, col in peers:
        pl.semaphore_signal(barrier, inc=1, device_id={"row": row, "col": col}, device_id_type=MESH)

    order_copy.wait()
    wanted = jnp.broadcast_to(order[...].astype(F32), (128, 256)).T
    source = lax.broadcasted_iota(jnp.int32, (256, 128), 1)
    for b in range(2):
        match = (source * 2 + b).astype(F32) == wanted
        sel[:, b * 128 : b * 128 + 128] = jnp.where(match, 1.0, 0.0).astype(BF16)
    lanes[...] = one_hot((256, 256), lambda row: (row & 127) * 2 + (row >> 7))
    frame_rows[...] = one_hot((256, 256), lambda row: (row & 15) * 16 + (row >> 4))
    rows32[...] = jnp.zeros_like(rows32)
    slopes[...] = jnp.zeros_like(slopes)

    filt_copy.wait()
    filt32[...] = filt[...].astype(F32)

    def centroid(n, carry):
        pix_copy(n).wait()
        for lane in range(4):
            low, high = lane * 128, min(lane * 128 + 128, SUBS)
            width = high - low

            def add(p, sums):
                rows = pl.ds(pl.multiple_of(p * 16, 16), 16)
                fx = filt32[0, rows, low:high]
                fy = filt32[1, rows, low:high]
                new = []
                for f in range(CHUNK_FRAMES):
                    v = pix[n * CHUNK_FRAMES + f, rows, low:high].astype(F32)
                    vx, vy = v * fx, v * fy
                    s, sx, sy = sums[3 * f : 3 * f + 3]
                    new += [s + (v[:8] + v[8:]), sx + (vx[:8] + vx[8:]), sy + (vy[:8] + vy[8:])]
                return tuple(new)

            zero = jnp.zeros((8, width), F32)
            sums = lax.fori_loop(0, PIX // 16, add, (zero,) * (3 * CHUNK_FRAMES))

            def total(kind):
                return jnp.concatenate(
                    [jnp.sum(sums[3 * f + kind], axis=0, keepdims=True) for f in range(CHUNK_FRAMES)], axis=0
                )

            flux = total(0)
            frames = pl.ds(pl.multiple_of(n * CHUNK_FRAMES, 8), CHUNK_FRAMES)
            slopes[0, frames, low:high] = total(1) / flux
            slopes[1, frames, low:high] = total(2) / flux
        return carry

    lax.fori_loop(0, PIX_CHUNKS, centroid, 0)

    parts = []
    for b in range(2):
        kinds = [slopes[k] if b == 0 else pltpu.roll(slopes[k], 512 - HALF, 1) for k in range(2)]
        for h in range(2):
            parts.append(jnp.concatenate([v[:, h * 128 : h * 128 + 128] for v in kinds], axis=1))
    raw = jnp.concatenate(parts, axis=0).astype(BF16)
    raw = jnp.dot(raw, lanes[...], preferred_element_type=F32)

    for b in range(2):
        for h in range(2):
            for q in range(2):
                first = b * 128 + h * 64
                rows32[pl.ds(h * 8 + b * 2 + q, FRAMES, stride=16), :] = raw[
                    first : first + FRAMES, q * 128 : q * 128 + 128
                ]
    by_piece[...] = rows32[...].reshape(DEVICES, 8, 128).astype(BF16)

    pl.semaphore_wait(barrier, DEVICES - 1)

    def remote(src, dst, send, recv, device):
        return pltpu.make_async_remote_copy(
            src_ref=src, dst_ref=dst, send_sem=send, recv_sem=recv, device_id=device, device_id_type=MESH
        )

    for row, col in peers:
        remote(
            by_piece.at[row * COLS + col], at_mid.at[rank], spread_send, spread_recv, {"row": row, "col": col}
        ).start()
    at_mid[rank] = by_piece[rank]
    for n in range(R_CHUNKS):
        right_copy(n).start()
    others = pl.ds(0, DEVICES - 1)
    spread = remote(by_piece.at[others], at_mid.at[others], spread_send, spread_recv, {"row": r})
    spread.wait_recv()
    rows32[...] = at_mid[...].astype(F32).reshape(DEVICES * 8, 128)
    every = jnp.concatenate(
        [
            jnp.concatenate([rows32[pl.ds(b * 2 + q, DEVICES, stride=8), :] for q in range(2)], axis=1)
            for b in range(2)
        ],
        axis=0,
    ).astype(BF16)
    by_col[...] = permute(sel[...], every).reshape(COLS, SPAN_J, 256)

    for row, col in peers:
        remote(by_col.at[col], gathered.at[rank], gather_send, gather_recv, {"row": row, "col": col}).start()
    gathered[rank] = by_col[c]
    for n in range(SPAN_I):
        left_copy(n).start()
    ranks_copy.wait()
    gather = remote(gathered.at[others], gathered.at[others], gather_send, gather_recv, {"row": r})
    gather.wait_recv()

    for g in range(FRAMES // 16):
        for h in range(2):
            rows = jnp.concatenate([gathered[2 * (g * 16 + f) + h] for f in range(16)], axis=0)
            pieces[:, g * 16 : g * 16 + 16, h * 256 : h * 256 + 256] = permute(frame_rows[...], rows).reshape(
                SPAN_J, 16, 256
            )

    lane_id = lax.broadcasted_iota(jnp.int32, (FRAMES, 128), 1)
    low_half = lane_id < RANK
    component = lane_id & (RANK - 1)

    def project(n, carry):
        right_copy(n).wait()
        for q in range(CHUNK_PAIRS):
            pair = n * CHUNK_PAIRS + q
            halves = []
            for e in range(2):
                piece = pieces[2 * pair + e]
                factors = right[:, 2 * pair + e].reshape(SPAN_I * RANK, TILE)
                halves.append(
                    lax.dot_general(
                        piece[:, :TILE], factors, (((1,), (1,)), ((), ())), preferred_element_type=F32
                    )
                )
            for i2 in range(SPAN_I // 2):
                kept = []
                for e in range(2):
                    bound = jnp.where(
                        low_half, ranks[2 * i2, 2 * pair + e], ranks[2 * i2 + 1, 2 * pair + e]
                    )
                    kept.append(jnp.where(component < bound, halves[e][:, i2 * 128 : i2 * 128 + 128], 0.0))
                proj[2 * i2, pair] = jnp.where(low_half, kept[0], pltpu.roll(kept[1], RANK, 1)).astype(BF16)
                proj[2 * i2 + 1, pair] = jnp.where(low_half, pltpu.roll(kept[0], RANK, 1), kept[1]).astype(BF16)
        return carry

    lax.fori_loop(0, R_CHUNKS, project, 0)

    for n in range(SPAN_I):
        left_copy(n).wait()

    def half_copy(s):
        return remote(
            other_half.at[s], half_in.at[s], c1_send.at[s], c1_recv.at[s], {"row": r, "col": c + 1 - 2 * core}
        )

    def tile_of(s):
        return lax.rem(z_hi + 1 - s // 4, 2) * 4 + lax.rem(y + 1 + s, 4)

    def chunk_copy(s):
        return remote(
            chunk_out.at[s], chunk_in.at[s], c2_send.at[s], c2_recv.at[s], {"row": r, "col": 2 * tile_of(s) + core}
        )

    def finish(s):
        half_copy(s).wait_recv()
        chunk_out[s] = (my_half[s] + half_in[s]).astype(BF16)
        chunk_copy(s).start()

    def command(s, carry):
        i = tile_of(s)
        lhs = jnp.concatenate([proj[i, q] for q in range(PAIRS)], axis=1)
        full = jnp.dot(lhs, left[i].reshape(SPAN_J * RANK, TILE), preferred_element_type=F32)
        lower, upper = full[:, :HALF], full[:, HALF:]
        first = core == 0
        my_half[s] = jnp.where(first, lower, upper)
        other_half[s] = jnp.where(first, upper, lower)
        half_copy(s).start()

        @pl.when(s >= 1)
        def _():
            finish(s - 1)

        return carry

    lax.fori_loop(0, SPAN_I, command, 0)
    last = SPAN_I - 1
    half_copy(last).wait_recv()
    total_cmd = my_half[last] + half_in[last]
    for s in range(last):
        chunk_copy(s).wait_recv()
        total_cmd += chunk_in[s].astype(F32)
    out_ref[...] = total_cmd

    spread.wait_send()
    gather.wait_send()
    for s in range(SPAN_I):
        half_copy(s).wait_send()
    for s in range(last):
        chunk_copy(s).wait_send()


def shards(pixels, match_filter, tile_ranks, column_order, right_factors, left_factors):
    hbm = pl.BlockSpec(memory_space=pltpu.HBM)
    dma = pltpu.SemaphoreType.DMA
    return pl.pallas_call(
        kernel,
        out_shape=jax.ShapeDtypeStruct((FRAMES, HALF), F32),
        in_specs=[hbm] * 6,
        out_specs=pl.BlockSpec(memory_space=pltpu.VMEM),
        scratch_shapes=[
            pltpu.VMEM((1, 256), jnp.int32),
            pltpu.SMEM((SPAN_I, SPAN_J), jnp.int32),
            pltpu.VMEM((FRAMES, PIX, SUBS), BF16),
            pltpu.VMEM((2, PIX, SUBS), BF16),
            pltpu.VMEM((2, PIX, SUBS), F32),
            pltpu.VMEM((SPAN_I, SPAN_J, RANK, TILE), BF16),
            pltpu.VMEM((SPAN_I, SPAN_J, RANK, TILE), BF16),
            pltpu.VMEM((2, FRAMES, 512), F32),
            pltpu.VMEM((256, 256), BF16),
            pltpu.VMEM((256, 256), BF16),
            pltpu.VMEM((256, 256), BF16),
            pltpu.VMEM((DEVICES * 8, 128), F32),
            pltpu.VMEM((DEVICES, 8, 128), BF16),
            pltpu.VMEM((DEVICES, 8, 128), BF16),
            pltpu.VMEM((COLS, SPAN_J, 256), BF16),
            pltpu.VMEM((DEVICES, SPAN_J, 256), BF16),
            pltpu.VMEM((SPAN_J, FRAMES, 512), BF16),
            pltpu.VMEM((SPAN_I, PAIRS, FRAMES, 128), BF16),
            pltpu.VMEM((SPAN_I, FRAMES, HALF), F32),
            pltpu.VMEM((SPAN_I, FRAMES, HALF), F32),
            pltpu.VMEM((SPAN_I, FRAMES, HALF), F32),
            pltpu.VMEM((SPAN_I - 1, FRAMES, HALF), BF16),
            pltpu.VMEM((SPAN_I - 1, FRAMES, HALF), BF16),
            dma, dma, dma, dma((PIX_CHUNKS,)), dma((R_CHUNKS,)), dma((SPAN_I,)),
            dma, dma, dma, dma,
            dma((SPAN_I,)), dma((SPAN_I,)),
            dma((SPAN_I - 1,)), dma((SPAN_I - 1,)),
        ],
        compiler_params=pltpu.CompilerParams(
            collective_id=0, has_side_effects=True, vmem_limit_bytes=64 * 1024 * 1024 - 65536
        ),
        name="frames_to_commands",
    )(
        column_order.reshape(1, -1),
        tile_ranks,
        jnp.transpose(pixels, (0, 2, 1)),
        jnp.transpose(match_filter, (1, 2, 0)),
        right_factors,
        left_factors,
    )


def solution(mesh):
    in_specs = (
        P(None, ("row", "col"), None),
        P(("row", "col"), None, None),
        P("row", "col"),
        P(),
        P("row", "col", None, None),
        P("row", "col", None, None),
    )
    out_specs = P(None, ("row", "col"))
    return jax.shard_map(shards, mesh=mesh, in_specs=in_specs, out_specs=out_specs, check_vma=False)
```

time: 58 us -> 53.1 us (0.916)
  Pallas kernels: 54.8 us -> 51.5 us
  local copies, waits for them, and re-layouts: 2.96 us -> 1.47 us
    pallas_call x1, Pallas kernels: 54.8 us -> 51.5 us  [shards(): pl.pallas_call(kernel, out_shape=jax.ShapeDtypeStruct((FRAMES, HALF), F32...]
    unnamed x7 -> x1, local copies, waits for them, and re-layouts: 2.96 us -> 1.47 us
where the time goes in v2:
time: 53.1 us; the launch traced here: 53 us
  Pallas kernels  51.5 us (97%)
  local copies, waits for them, and re-layouts  1.47 us (3%)
    pallas_call x1, Pallas kernels, shards(): pl.pallas_call(kernel, out_shape=jax.ShapeDtypeStruct((FRAMES, HALF), F32...  51.5 us
    unnamed x1, local copies, waits for them, and re-layouts  1.47 us

profile of v2, /device:TPU:1, one launch (start us, length us, event | category | flops | bytes accessed | tf_op | source)
XLA Modules:
  0.0 53.0 jit_solution(6995335126104541649)
XLA Ops:
  0.0 51.5 %frames_to_commands.1 = f32[64,250]{1,0:T(8,128)} custom-call(s32[1,256]{1,0:T(1,128)} %bitcast.5, s32[8,16]{1,0:T(8,128)} %ranks_hbm.1, bf16[64,144,500]{2,1,0:T(8,128)(2,1)} %bitcast.3, bf16[2,144,500]{2,1,0:T(8,128)(2,1)} %bitcast.4, bf16[8,16,64,500]{3,2,1,0:T(8,128)(2,1)} %right_hbm.1, bf16[8,16,64,500]{3,2,1,0:T(8,128)(2,1)} %left_hbm.1), custom_call_target="tpu_custom_call" | custom-call | tf_op jit(solution)/shard_map/frames_to_commands/pallas_call | solution.py:282
  51.5 1.5 %copy.8 = f32[64,250]{1,0:T(8,128)} copy(f32[64,250]{1,0:T(8,128)} %frames_to_commands.1) | data formatting | bytes 128000

commit v3 on v2

--- a/solution.py
+++ b/solution.py
@@ -34,7 +34,7 @@
 
 def kernel(
     order_hbm, ranks_hbm, pix_hbm, filt_hbm, right_hbm, left_hbm, out_ref,
-    order, ranks, pix, filt, filt32, right, left, slopes, sel, lanes, frame_rows, rows32, by_piece, at_mid, by_col, gathered,
+    order, ranks, pix, filt, filt32, right, left, slopes, sel, lanes, frame_rows, rows32, folds, by_piece, at_mid, by_col, gathered,
     pieces, proj, other_half, my_half, half_in, chunk_out, chunk_in,
     order_sem, ranks_sem, filt_sem, pix_sem, right_sem, left_sem,
     spread_send, spread_recv, gather_send, gather_recv,
@@ -91,9 +91,10 @@
         match = (source * 2 + b).astype(F32) == wanted
         sel[:, b * 128 : b * 128 + 128] = jnp.where(match, 1.0, 0.0).astype(BF16)
     lanes[...] = one_hot((256, 256), lambda row: (row & 127) * 2 + (row >> 7))
-    frame_rows[...] = one_hot((256, 256), lambda row: (row & 15) * 16 + (row >> 4))
+    frame_rows[...] = one_hot((256, 256), lambda row: (row & 31) * 8 + (row >> 5))
     rows32[...] = jnp.zeros_like(rows32)
     slopes[...] = jnp.zeros_like(slopes)
+    folds[...] = jnp.zeros_like(folds)
 
     filt_copy.wait()
     filt32[...] = filt[...].astype(F32)
@@ -104,25 +105,25 @@
             low, high = lane * 128, min(lane * 128 + 128, SUBS)
             width = high - low
 
-            def add(p, sums):
-                rows = pl.ds(pl.multiple_of(p * 16, 16), 16)
-                fx = filt32[0, rows, low:high]
-                fy = filt32[1, rows, low:high]
-                new = []
+            zero = jnp.zeros((8, width), F32)
+            sums = [[zero] * CHUNK_FRAMES for _ in range(3)]
+            for p in range(0, PIX, 16):
+                fx = filt32[0, p : p + 16, low:high]
+                fy = filt32[1, p : p + 16, low:high]
                 for f in range(CHUNK_FRAMES):
-                    v = pix[n * CHUNK_FRAMES + f, rows, low:high].astype(F32)
+                    v = pix[n * CHUNK_FRAMES + f, p : p + 16, low:high].astype(F32)
                     vx, vy = v * fx, v * fy
-                    s, sx, sy = sums[3 * f : 3 * f + 3]
-                    new += [s + (v[:8] + v[8:]), sx + (vx[:8] + vx[8:]), sy + (vy[:8] + vy[8:])]
-                return tuple(new)
-
-            zero = jnp.zeros((8, width), F32)
-            sums = lax.fori_loop(0, PIX // 16, add, (zero,) * (3 * CHUNK_FRAMES))
+                    sums[0][f] = sums[0][f] + (v[:8] + v[8:])
+                    sums[1][f] = sums[1][f] + (vx[:8] + vx[8:])
+                    sums[2][f] = sums[2][f] + (vy[:8] + vy[8:])
+            for kind in range(3):
+                for f in range(CHUNK_FRAMES):
+                    first = (lane * 3 + kind) * 64 + f * 8
+                    folds[first : first + 8, :width] = sums[kind][f]
 
             def total(kind):
-                return jnp.concatenate(
-                    [jnp.sum(sums[3 * f + kind], axis=0, keepdims=True) for f in range(CHUNK_FRAMES)], axis=0
-                )
+                first = (lane * 3 + kind) * 64
+                return sum(folds[pl.ds(first + k, CHUNK_FRAMES, stride=8), :] for k in range(8))[:, :width]
 
             flux = total(0)
             frames = pl.ds(pl.multiple_of(n * CHUNK_FRAMES, 8), CHUNK_FRAMES)
@@ -174,56 +175,73 @@
         ],
         axis=0,
     ).astype(BF16)
-    by_col[...] = permute(sel[...], every).reshape(COLS, SPAN_J, 256)
-
-    for row, col in peers:
-        remote(by_col.at[col], gathered.at[rank], gather_send, gather_recv, {"row": row, "col": col}).start()
-    gathered[rank] = by_col[c]
+    chosen = jnp.dot(sel[...], every, preferred_element_type=F32).reshape(COLS, 2, SPAN_J // 2, 256)
+    for part in range(2):
+        by_col[part] = chosen[:, part].astype(BF16)
+
+    for part in range(2):
+        for row, col in peers:
+            remote(
+                by_col.at[part, col], gathered.at[part, rank], gather_send.at[part], gather_recv.at[part],
+                {"row": row, "col": col},
+            ).start()
+        gathered[part, rank] = by_col[part, c]
+    gather = [
+        remote(
+            gathered.at[part, others], gathered.at[part, others], gather_send.at[part], gather_recv.at[part],
+            {"row": r},
+        )
+        for part in range(2)
+    ]
     for n in range(SPAN_I):
         left_copy(n).start()
     ranks_copy.wait()
-    gather = remote(gathered.at[others], gathered.at[others], gather_send, gather_recv, {"row": r})
-    gather.wait_recv()
-
-    for g in range(FRAMES // 16):
-        for h in range(2):
-            rows = jnp.concatenate([gathered[2 * (g * 16 + f) + h] for f in range(16)], axis=0)
-            pieces[:, g * 16 : g * 16 + 16, h * 256 : h * 256 + 256] = permute(frame_rows[...], rows).reshape(
-                SPAN_J, 16, 256
-            )
+
+    def arrive(part):
+        right_copy(2 * part).wait()
+        right_copy(2 * part + 1).wait()
+        gather[part].wait_recv()
+        for g in range(2):
+            for h in range(2):
+                rows = jnp.concatenate(
+                    [gathered[part, 2 * (g * 32 + f) + h].astype(F32) for f in range(32)], axis=0
+                ).astype(BF16)
+                pieces[part * 8 : part * 8 + 8, g * 32 : g * 32 + 32, h * 256 : h * 256 + 256] = permute(
+                    frame_rows[...], rows
+                ).reshape(SPAN_J // 2, 32, 256)
 
     lane_id = lax.broadcasted_iota(jnp.int32, (FRAMES, 128), 1)
     low_half = lane_id < RANK
     component = lane_id & (RANK - 1)
 
-    def project(n, carry):
-        right_copy(n).wait()
+    def project(n, first):
         for q in range(CHUNK_PAIRS):
             pair = n * CHUNK_PAIRS + q
             halves = []
             for e in range(2):
-                piece = pieces[2 * pair + e]
-                factors = right[:, 2 * pair + e].reshape(SPAN_I * RANK, TILE)
+                factors = right[pl.ds(first, 4), 2 * pair + e].reshape(4 * RANK, TILE)
                 halves.append(
                     lax.dot_general(
-                        piece[:, :TILE], factors, (((1,), (1,)), ((), ())), preferred_element_type=F32
+                        pieces[2 * pair + e][:, :TILE], factors, (((1,), (1,)), ((), ())), preferred_element_type=F32
                     )
                 )
-            for i2 in range(SPAN_I // 2):
+            for i2 in range(2):
+                i = first + 2 * i2
                 kept = []
                 for e in range(2):
-                    bound = jnp.where(
-                        low_half, ranks[2 * i2, 2 * pair + e], ranks[2 * i2 + 1, 2 * pair + e]
-                    )
+                    bound = jnp.where(low_half, ranks[i, 2 * pair + e], ranks[i + 1, 2 * pair + e])
                     kept.append(jnp.where(component < bound, halves[e][:, i2 * 128 : i2 * 128 + 128], 0.0))
-                proj[2 * i2, pair] = jnp.where(low_half, kept[0], pltpu.roll(kept[1], RANK, 1)).astype(BF16)
-                proj[2 * i2 + 1, pair] = jnp.where(low_half, pltpu.roll(kept[0], RANK, 1), kept[1]).astype(BF16)
+                proj[i, pair] = jnp.where(low_half, kept[0], pltpu.roll(kept[1], RANK, 1)).astype(BF16)
+                proj[i + 1, pair] = jnp.where(low_half, pltpu.roll(kept[0], RANK, 1), kept[1]).astype(BF16)
+
+    def project_early(n, carry):
+        project(lax.rem(n, 2), n // 2 * 4)
         return carry
 
-    lax.fori_loop(0, R_CHUNKS, project, 0)
-
-    for n in range(SPAN_I):
-        left_copy(n).wait()
+    far, near = (1 - z_hi) * 4, z_hi * 4
+    arrive(0)
+    lax.fori_loop(0, 4, project_early, 0)
+    arrive(1)
 
     def half_copy(s):
         return remote(
@@ -253,13 +271,21 @@
         other_half[s] = jnp.where(first, upper, lower)
         half_copy(s).start()
 
-        @pl.when(s >= 1)
+        @pl.when(lax.rem(s, 4) > 0)
         def _():
             finish(s - 1)
 
         return carry
 
-    lax.fori_loop(0, SPAN_I, command, 0)
+    project(2, far)
+    project(3, far)
+    for n in range(SPAN_I):
+        left_copy(n).wait()
+    lax.fori_loop(0, 4, command, 0)
+    project(2, near)
+    finish(3)
+    project(3, near)
+    lax.fori_loop(4, SPAN_I, command, 0)
     last = SPAN_I - 1
     half_copy(last).wait_recv()
     total_cmd = my_half[last] + half_in[last]
@@ -269,7 +295,8 @@
     out_ref[...] = total_cmd
 
     spread.wait_send()
-    gather.wait_send()
+    for part in range(2):
+        gather[part].wait_send()
     for s in range(SPAN_I):
         half_copy(s).wait_send()
     for s in range(last):
@@ -297,10 +324,11 @@
             pltpu.VMEM((256, 256), BF16),
             pltpu.VMEM((256, 256), BF16),
             pltpu.VMEM((DEVICES * 8, 128), F32),
+            pltpu.VMEM((4 * 3 * 64, 128), F32),
             pltpu.VMEM((DEVICES, 8, 128), BF16),
             pltpu.VMEM((DEVICES, 8, 128), BF16),
-            pltpu.VMEM((COLS, SPAN_J, 256), BF16),
-            pltpu.VMEM((DEVICES, SPAN_J, 256), BF16),
+            pltpu.VMEM((2, COLS, SPAN_J // 2, 256), BF16),
+            pltpu.VMEM((2, DEVICES, SPAN_J // 2, 256), BF16),
             pltpu.VMEM((SPAN_J, FRAMES, 512), BF16),
             pltpu.VMEM((SPAN_I, PAIRS, FRAMES, 128), BF16),
             pltpu.VMEM((SPAN_I, FRAMES, HALF), F32),
@@ -309,7 +337,7 @@
             pltpu.VMEM((SPAN_I - 1, FRAMES, HALF), BF16),
             pltpu.VMEM((SPAN_I - 1, FRAMES, HALF), BF16),
             dma, dma, dma, dma((PIX_CHUNKS,)), dma((R_CHUNKS,)), dma((SPAN_I,)),
-            dma, dma, dma, dma,
+            dma, dma, dma((2,)), dma((2,)),
             dma((SPAN_I,)), dma((SPAN_I,)),
             dma((SPAN_I - 1,)), dma((SPAN_I - 1,)),
         ],

time: 53.1 us -> 48.9 us (0.921)
  Pallas kernels: 51.5 us -> 47.3 us
    pallas_call x1, Pallas kernels: 51.5 us -> 47.3 us  [shards(): pl.pallas_call(kernel, out_shape=jax.ShapeDtypeStruct((FRAMES, HALF), F32...]
where the time goes in v3:
time: 48.9 us; the launch traced here: 48.8 us
  Pallas kernels  47.3 us (97%)
  local copies, waits for them, and re-layouts  1.47 us (3%)
    pallas_call x1, Pallas kernels, shards(): pl.pallas_call(kernel, out_shape=jax.ShapeDtypeStruct((FRAMES, HALF), F32...  47.3 us
    unnamed x1, local copies, waits for them, and re-layouts  1.47 us

profile of v3, /device:TPU:1, one launch (start us, length us, event | category | flops | bytes accessed | tf_op | source)
XLA Modules:
  0.0 48.8 jit_solution(15390278821603603735)
XLA Ops:
  0.0 47.3 %frames_to_commands.1 = f32[64,250]{1,0:T(8,128)} custom-call(s32[1,256]{1,0:T(1,128)} %bitcast.5, s32[8,16]{1,0:T(8,128)} %ranks_hbm.1, bf16[64,144,500]{2,1,0:T(8,128)(2,1)} %bitcast.3, bf16[2,144,500]{2,1,0:T(8,128)(2,1)} %bitcast.4, bf16[8,16,64,500]{3,2,1,0:T(8,128)(2,1)} %right_hbm.1, bf16[8,16,64,500]{3,2,1,0:T(8,128)(2,1)} %left_hbm.1), custom_call_target="tpu_custom_call" | custom-call | tf_op jit(solution)/shard_map/frames_to_commands/pallas_call | solution.py:309
  47.3 1.5 %copy.8 = f32[64,250]{1,0:T(8,128)} copy(f32[64,250]{1,0:T(8,128)} %frames_to_commands.1) | data formatting | bytes 128000

commit v4 on v3

--- a/solution.py
+++ b/solution.py
@@ -55,11 +55,13 @@
     cores = [core, 1 - core]
     offsets = [(dx, dy, dz, dk) for dx in range(4) for dy in range(4) for dz in range(4) for dk in range(2)]
     offsets.sort(key=lambda o: -sum(min(d, 4 - d) for d in o[:3]))
-    peers = [
-        (xs[dx] * 2 + lax.rem(zs[dz], 2), (zs[dz] // 2 * 4 + ys[dy]) * 2 + cores[dk])
-        for dx, dy, dz, dk in offsets
-        if (dx, dy, dz, dk) != (0, 0, 0, 0)
-    ]
+    peers_at = {d: [] for d in range(4)}
+    peers = []
+    for dx, dy, dz, dk in offsets:
+        if (dx, dy, dz, dk) != (0, 0, 0, 0):
+            peer = (xs[dx] * 2 + lax.rem(zs[dz], 2), (zs[dz] // 2 * 4 + ys[dy]) * 2 + cores[dk])
+            peers.append(peer)
+            peers_at[dx].append(peer)
 
     def pix_copy(n):
         frames = pl.ds(n * CHUNK_FRAMES, CHUNK_FRAMES)
@@ -159,13 +161,13 @@
 
     for row, col in peers:
         remote(
-            by_piece.at[row * COLS + col], at_mid.at[rank], spread_send, spread_recv, {"row": row, "col": col}
+            by_piece.at[row * COLS + col, pl.ds(0, 4)], at_mid.at[rank, pl.ds(0, 4)], spread_send, spread_recv, {"row": row, "col": col}
         ).start()
     at_mid[rank] = by_piece[rank]
     for n in range(R_CHUNKS):
         right_copy(n).start()
     others = pl.ds(0, DEVICES - 1)
-    spread = remote(by_piece.at[others], at_mid.at[others], spread_send, spread_recv, {"row": r})
+    spread = remote(by_piece.at[others, pl.ds(0, 4)], at_mid.at[others, pl.ds(0, 4)], spread_send, spread_recv, {"row": r})
     spread.wait_recv()
     rows32[...] = at_mid[...].astype(F32).reshape(DEVICES * 8, 128)
     every = jnp.concatenate(
@@ -179,20 +181,39 @@
     for part in range(2):
         by_col[part] = chosen[:, part].astype(BF16)
 
-    for part in range(2):
-        for row, col in peers:
+    def gather_to(part, dx):
+        for row, col in peers_at[dx]:
             remote(
-                by_col.at[part, col], gathered.at[part, rank], gather_send.at[part], gather_recv.at[part],
+                by_col.at[part, col], gathered.at[part, rank], gather_send.at[part, dx], gather_recv.at[part, dx],
                 {"row": row, "col": col},
             ).start()
-        gathered[part, rank] = by_col[part, c]
-    gather = [
-        remote(
-            gathered.at[part, others], gathered.at[part, others], gather_send.at[part], gather_recv.at[part],
+
+    def gathered_at(part, dx):
+        slots = pl.ds(0, len(peers_at[dx]))
+        return remote(
+            gathered.at[part, slots], gathered.at[part, slots], gather_send.at[part, dx], gather_recv.at[part, dx],
             {"row": r},
         )
-        for part in range(2)
-    ]
+
+    def relay(part):
+        slots = pl.ds(xs[3 if part == 0 else 1] * 32, 32)
+        return remote(
+            gathered.at[part, slots], gathered.at[part, slots], gather_send.at[part, 2], gather_recv.at[part, 2],
+            {"row": xs[1 if part == 0 else 3] * 2 + lax.rem(r, 2), "col": c},
+        )
+
+    gather_to(0, 1)
+    gather_to(1, 3)
+    gather_to(0, 3)
+    gather_to(0, 0)
+    gathered[0, rank] = by_col[0, c]
+    gathered_at(0, 1).wait_recv()
+    relay(0).start()
+    gather_to(1, 1)
+    gathered_at(1, 3).wait_recv()
+    relay(1).start()
+    gather_to(1, 0)
+    gathered[1, rank] = by_col[1, c]
     for n in range(SPAN_I):
         left_copy(n).start()
     ranks_copy.wait()
@@ -200,7 +221,9 @@
     def arrive(part):
         right_copy(2 * part).wait()
         right_copy(2 * part + 1).wait()
-        gather[part].wait_recv()
+        gathered_at(part, 3 if part == 0 else 1).wait_recv()
+        gathered_at(part, 0).wait_recv()
+        relay(part).wait_recv()
         for g in range(2):
             for h in range(2):
                 rows = jnp.concatenate(
@@ -261,31 +284,35 @@
         chunk_out[s] = (my_half[s] + half_in[s]).astype(BF16)
         chunk_copy(s).start()
 
-    def command(s, carry):
-        i = tile_of(s)
-        lhs = jnp.concatenate([proj[i, q] for q in range(PAIRS)], axis=1)
-        full = jnp.dot(lhs, left[i].reshape(SPAN_J * RANK, TILE), preferred_element_type=F32)
-        lower, upper = full[:, :HALF], full[:, HALF:]
+    def commands(steps):
+        full = []
+        for s in steps:
+            i = tile_of(s)
+            lhs = jnp.concatenate([proj[i, q] for q in range(PAIRS)], axis=1)
+            full.append(jnp.dot(lhs, left[i].reshape(SPAN_J * RANK, TILE), preferred_element_type=F32))
         first = core == 0
-        my_half[s] = jnp.where(first, lower, upper)
-        other_half[s] = jnp.where(first, upper, lower)
-        half_copy(s).start()
-
-        @pl.when(lax.rem(s, 4) > 0)
-        def _():
-            finish(s - 1)
-
-        return carry
+        for s, tile in zip(steps, full):
+            lower, upper = tile[:, :HALF], tile[:, HALF:]
+            other_half[s] = jnp.where(first, upper, lower)
+            my_half[s] = jnp.where(first, lower, upper)
+            half_copy(s).start()
 
     project(2, far)
     project(3, far)
     for n in range(SPAN_I):
         left_copy(n).wait()
-    lax.fori_loop(0, 4, command, 0)
+    commands((0, 1))
+    commands((2, 3))
+    finish(0)
+    finish(1)
     project(2, near)
+    finish(2)
     finish(3)
     project(3, near)
-    lax.fori_loop(4, SPAN_I, command, 0)
+    commands((4, 5))
+    commands((6, 7))
+    for s in range(4, 7):
+        finish(s)
     last = SPAN_I - 1
     half_copy(last).wait_recv()
     total_cmd = my_half[last] + half_in[last]
@@ -296,7 +323,9 @@
 
     spread.wait_send()
     for part in range(2):
-        gather[part].wait_send()
+        for dx in (0, 1, 3):
+            gathered_at(part, dx).wait_send()
+        relay(part).wait_send()
     for s in range(SPAN_I):
         half_copy(s).wait_send()
     for s in range(last):
@@ -337,7 +366,7 @@
             pltpu.VMEM((SPAN_I - 1, FRAMES, HALF), BF16),
             pltpu.VMEM((SPAN_I - 1, FRAMES, HALF), BF16),
             dma, dma, dma, dma((PIX_CHUNKS,)), dma((R_CHUNKS,)), dma((SPAN_I,)),
-            dma, dma, dma((2,)), dma((2,)),
+            dma, dma, dma((2, 4)), dma((2, 4)),
             dma((SPAN_I,)), dma((SPAN_I,)),
             dma((SPAN_I - 1,)), dma((SPAN_I - 1,)),
         ],

time: 48.9 us -> 46.7 us (0.955)
  Pallas kernels: 47.3 us -> 45.1 us
    pallas_call x1, Pallas kernels: 47.3 us -> 45.1 us  [shards(): pl.pallas_call(kernel, out_shape=jax.ShapeDtypeStruct((FRAMES, HALF), F32...]
where the time goes in v4:
time: 46.7 us; the launch traced here: 46.5 us
  Pallas kernels  45.1 us (97%)
  local copies, waits for them, and re-layouts  1.47 us (3%)
    pallas_call x1, Pallas kernels, shards(): pl.pallas_call(kernel, out_shape=jax.ShapeDtypeStruct((FRAMES, HALF), F32...  45.1 us
    unnamed x1, local copies, waits for them, and re-layouts  1.47 us

profile of v4, /device:TPU:1, one launch (start us, length us, event | category | flops | bytes accessed | tf_op | source)
XLA Modules:
  0.0 46.5 jit_solution(9315336655278971249)
XLA Ops:
  0.0 45.1 %frames_to_commands.1 = f32[64,250]{1,0:T(8,128)} custom-call(s32[1,256]{1,0:T(1,128)} %bitcast.5, s32[8,16]{1,0:T(8,128)} %ranks_hbm.1, bf16[64,144,500]{2,1,0:T(8,128)(2,1)} %bitcast.3, bf16[2,144,500]{2,1,0:T(8,128)(2,1)} %bitcast.4, bf16[8,16,64,500]{3,2,1,0:T(8,128)(2,1)} %right_hbm.1, bf16[8,16,64,500]{3,2,1,0:T(8,128)(2,1)} %left_hbm.1), custom_call_target="tpu_custom_call" | custom-call | tf_op jit(solution)/shard_map/frames_to_commands/pallas_call | solution.py:338
  45.1 1.5 %copy.8 = f32[64,250]{1,0:T(8,128)} copy(f32[64,250]{1,0:T(8,128)} %frames_to_commands.1) | data formatting | bytes 128000

commit v5 on v4

--- a/solution.py
+++ b/solution.py
@@ -35,10 +35,10 @@
 def kernel(
     order_hbm, ranks_hbm, pix_hbm, filt_hbm, right_hbm, left_hbm, out_ref,
     order, ranks, pix, filt, filt32, right, left, slopes, sel, lanes, frame_rows, rows32, folds, by_piece, at_mid, by_col, gathered,
-    pieces, proj, other_half, my_half, half_in, chunk_out, chunk_in,
+    pieces, proj, other_half, my_half, early, half_in, chunk_out, chunk_in, direct_out, direct_in,
     order_sem, ranks_sem, filt_sem, pix_sem, right_sem, left_sem,
     spread_send, spread_recv, gather_send, gather_recv,
-    c1_send, c1_recv, c2_send, c2_recv,
+    c1_send, c1_recv, c2_send, c2_recv, direct_send, direct_recv,
 ):
     r = lax.axis_index("row")
     c = lax.axis_index("col")
@@ -86,15 +86,7 @@
     for row, col in peers:
         pl.semaphore_signal(barrier, inc=1, device_id={"row": row, "col": col}, device_id_type=MESH)
 
-    order_copy.wait()
-    wanted = jnp.broadcast_to(order[...].astype(F32), (128, 256)).T
-    source = lax.broadcasted_iota(jnp.int32, (256, 128), 1)
-    for b in range(2):
-        match = (source * 2 + b).astype(F32) == wanted
-        sel[:, b * 128 : b * 128 + 128] = jnp.where(match, 1.0, 0.0).astype(BF16)
     lanes[...] = one_hot((256, 256), lambda row: (row & 127) * 2 + (row >> 7))
-    frame_rows[...] = one_hot((256, 256), lambda row: (row & 31) * 8 + (row >> 5))
-    rows32[...] = jnp.zeros_like(rows32)
     slopes[...] = jnp.zeros_like(slopes)
     folds[...] = jnp.zeros_like(folds)
 
@@ -164,6 +156,13 @@
             by_piece.at[row * COLS + col, pl.ds(0, 4)], at_mid.at[rank, pl.ds(0, 4)], spread_send, spread_recv, {"row": row, "col": col}
         ).start()
     at_mid[rank] = by_piece[rank]
+    order_copy.wait()
+    wanted = jnp.broadcast_to(order[...].astype(F32), (128, 256)).T
+    source = lax.broadcasted_iota(jnp.int32, (256, 128), 1)
+    for b in range(2):
+        match = (source * 2 + b).astype(F32) == wanted
+        sel[:, b * 128 : b * 128 + 128] = jnp.where(match, 1.0, 0.0).astype(BF16)
+    frame_rows[...] = one_hot((256, 256), lambda row: (row & 31) * 8 + (row >> 5))
     for n in range(R_CHUNKS):
         right_copy(n).start()
     others = pl.ds(0, DEVICES - 1)
@@ -207,13 +206,13 @@
     gather_to(0, 3)
     gather_to(0, 0)
     gathered[0, rank] = by_col[0, c]
+    gather_to(1, 1)
     gathered_at(0, 1).wait_recv()
     relay(0).start()
-    gather_to(1, 1)
+    gather_to(1, 0)
+    gathered[1, rank] = by_col[1, c]
     gathered_at(1, 3).wait_recv()
     relay(1).start()
-    gather_to(1, 0)
-    gathered[1, rank] = by_col[1, c]
     for n in range(SPAN_I):
         left_copy(n).start()
     ranks_copy.wait()
@@ -257,13 +256,19 @@
                 proj[i, pair] = jnp.where(low_half, kept[0], pltpu.roll(kept[1], RANK, 1)).astype(BF16)
                 proj[i + 1, pair] = jnp.where(low_half, pltpu.roll(kept[0], RANK, 1), kept[1]).astype(BF16)
 
-    def project_early(n, carry):
-        project(lax.rem(n, 2), n // 2 * 4)
-        return carry
+    def tile_product(i, start, stop):
+        lhs = jnp.concatenate([proj[i, q] for q in range(start, stop)], axis=1)
+        factors = left[i, 2 * start : 2 * stop].reshape(2 * (stop - start) * RANK, TILE)
+        return jnp.dot(lhs, factors, preferred_element_type=F32)
 
     far, near = (1 - z_hi) * 4, z_hi * 4
     arrive(0)
-    lax.fori_loop(0, 4, project_early, 0)
+    project(0, far)
+    project(1, far)
+    for n in range(SPAN_I):
+        left_copy(n).wait()
+    for k in range(4):
+        early[k] = tile_product(far + k, 0, PAIRS // 2)
     arrive(1)
 
     def half_copy(s):
@@ -272,11 +277,16 @@
         )
 
     def tile_of(s):
-        return lax.rem(z_hi + 1 - s // 4, 2) * 4 + lax.rem(y + 1 + s, 4)
+        return lax.rem(z_hi + 1 - s // 4, 2) * 4 + ys[(2, 1, 3, 0)[s % 4]]
 
     def chunk_copy(s):
         return remote(
             chunk_out.at[s], chunk_in.at[s], c2_send.at[s], c2_recv.at[s], {"row": r, "col": 2 * tile_of(s) + core}
+        )
+
+    def direct_copy():
+        return remote(
+            direct_out, direct_in, direct_send, direct_recv, {"row": r, "col": 2 * tile_of(6) + 1 - core}
         )
 
     def finish(s):
@@ -288,37 +298,47 @@
         full = []
         for s in steps:
             i = tile_of(s)
-            lhs = jnp.concatenate([proj[i, q] for q in range(PAIRS)], axis=1)
-            full.append(jnp.dot(lhs, left[i].reshape(SPAN_J * RANK, TILE), preferred_element_type=F32))
+            if s < 4:
+                full.append(early[i - far] + tile_product(i, PAIRS // 2, PAIRS))
+            else:
+                full.append(tile_product(i, 0, PAIRS))
         first = core == 0
         for s, tile in zip(steps, full):
             lower, upper = tile[:, :HALF], tile[:, HALF:]
             other_half[s] = jnp.where(first, upper, lower)
             my_half[s] = jnp.where(first, lower, upper)
-            half_copy(s).start()
+            if s == 6:
+                chunk_out[s] = my_half[s].astype(BF16)
+                chunk_copy(s).start()
+                direct_out[...] = other_half[s].astype(BF16)
+                direct_copy().start()
+            else:
+                half_copy(s).start()
 
     project(2, far)
     project(3, far)
-    for n in range(SPAN_I):
-        left_copy(n).wait()
     commands((0, 1))
     commands((2, 3))
+    project(0, near)
     finish(0)
     finish(1)
-    project(2, near)
+    project(1, near)
     finish(2)
     finish(3)
+    project(2, near)
     project(3, near)
     commands((4, 5))
     commands((6, 7))
-    for s in range(4, 7):
-        finish(s)
+    finish(4)
+    finish(5)
     last = SPAN_I - 1
     half_copy(last).wait_recv()
     total_cmd = my_half[last] + half_in[last]
     for s in range(last):
         chunk_copy(s).wait_recv()
         total_cmd += chunk_in[s].astype(F32)
+    direct_copy().wait_recv()
+    total_cmd += direct_in[...].astype(F32)
     out_ref[...] = total_cmd
 
     spread.wait_send()
@@ -326,8 +346,9 @@
         for dx in (0, 1, 3):
             gathered_at(part, dx).wait_send()
         relay(part).wait_send()
-    for s in range(SPAN_I):
+    for s in (0, 1, 2, 3, 4, 5, 7):
         half_copy(s).wait_send()
+    direct_copy().wait_send()
     for s in range(last):
         chunk_copy(s).wait_send()
 
@@ -362,13 +383,16 @@
             pltpu.VMEM((SPAN_I, PAIRS, FRAMES, 128), BF16),
             pltpu.VMEM((SPAN_I, FRAMES, HALF), F32),
             pltpu.VMEM((SPAN_I, FRAMES, HALF), F32),
+            pltpu.VMEM((4, FRAMES, TILE), F32),
             pltpu.VMEM((SPAN_I, FRAMES, HALF), F32),
             pltpu.VMEM((SPAN_I - 1, FRAMES, HALF), BF16),
             pltpu.VMEM((SPAN_I - 1, FRAMES, HALF), BF16),
+            pltpu.VMEM((FRAMES, HALF), BF16),
+            pltpu.VMEM((FRAMES, HALF), BF16),
             dma, dma, dma, dma((PIX_CHUNKS,)), dma((R_CHUNKS,)), dma((SPAN_I,)),
             dma, dma, dma((2, 4)), dma((2, 4)),
             dma((SPAN_I,)), dma((SPAN_I,)),
-            dma((SPAN_I - 1,)), dma((SPAN_I - 1,)),
+            dma((SPAN_I - 1,)), dma((SPAN_I - 1,)), dma, dma,
         ],
         compiler_params=pltpu.CompilerParams(
             collective_id=0, has_side_effects=True, vmem_limit_bytes=64 * 1024 * 1024 - 65536

time: 46.7 us -> 44 us (0.942)
  Pallas kernels: 45.1 us -> 42.3 us
    pallas_call x1, Pallas kernels: 45.1 us -> 42.3 us  [shards(): pl.pallas_call(kernel, out_shape=jax.ShapeDtypeStruct((FRAMES, HALF), F32...]
where the time goes in v5:
time: 44 us; the launch traced here: 43.8 us
  Pallas kernels  42.3 us (96%)
  local copies, waits for them, and re-layouts  1.47 us (3%)
    pallas_call x1, Pallas kernels, shards(): pl.pallas_call(kernel, out_shape=jax.ShapeDtypeStruct((FRAMES, HALF), F32...  42.3 us
    unnamed x1, local copies, waits for them, and re-layouts  1.47 us

profile of v5, /device:TPU:1, one launch (start us, length us, event | category | flops | bytes accessed | tf_op | source)
XLA Modules:
  0.0 43.8 jit_solution(3081116627993935832)
XLA Ops:
  0.0 42.3 %frames_to_commands.1 = f32[64,250]{1,0:T(8,128)} custom-call(s32[1,256]{1,0:T(1,128)} %bitcast.5, s32[8,16]{1,0:T(8,128)} %ranks_hbm.1, bf16[64,144,500]{2,1,0:T(8,128)(2,1)} %bitcast.3, bf16[2,144,500]{2,1,0:T(8,128)(2,1)} %bitcast.4, bf16[8,16,64,500]{3,2,1,0:T(8,128)(2,1)} %right_hbm.1, bf16[8,16,64,500]{3,2,1,0:T(8,128)(2,1)} %left_hbm.1), custom_call_target="tpu_custom_call" | custom-call | tf_op jit(solution)/shard_map/frames_to_commands/pallas_call | solution.py:359
  42.3 1.5 %copy.8 = f32[64,250]{1,0:T(8,128)} copy(f32[64,250]{1,0:T(8,128)} %frames_to_commands.1) | data formatting | bytes 128000

commit v6 on v5

--- a/solution.py
+++ b/solution.py
@@ -269,6 +269,8 @@
         left_copy(n).wait()
     for k in range(4):
         early[k] = tile_product(far + k, 0, PAIRS // 2)
+    project(0, near)
+    project(1, near)
     arrive(1)
 
     def half_copy(s):
@@ -319,14 +321,12 @@
     project(3, far)
     commands((0, 1))
     commands((2, 3))
-    project(0, near)
+    project(2, near)
     finish(0)
     finish(1)
-    project(1, near)
+    project(3, near)
     finish(2)
     finish(3)
-    project(2, near)
-    project(3, near)
     commands((4, 5))
     commands((6, 7))
     finish(4)

time: 44 us -> 43.9 us (level)
  no operation moved by 1% of the time
where the time goes in v6:
time: 43.9 us; the launch traced here: 43.7 us
  Pallas kernels  42.2 us (96%)
  local copies, waits for them, and re-layouts  1.47 us (3%)
    pallas_call x1, Pallas kernels, shards(): pl.pallas_call(kernel, out_shape=jax.ShapeDtypeStruct((FRAMES, HALF), F32...  42.2 us
    unnamed x1, local copies, waits for them, and re-layouts  1.47 us

profile of v6, /device:TPU:1, one launch (start us, length us, event | category | flops | bytes accessed | tf_op | source)
XLA Modules:
  0.0 43.7 jit_solution(10611127694514713874)
XLA Ops:
  0.0 42.2 %frames_to_commands.1 = f32[64,250]{1,0:T(8,128)} custom-call(s32[1,256]{1,0:T(1,128)} %bitcast.5, s32[8,16]{1,0:T(8,128)} %ranks_hbm.1, bf16[64,144,500]{2,1,0:T(8,128)(2,1)} %bitcast.3, bf16[2,144,500]{2,1,0:T(8,128)(2,1)} %bitcast.4, bf16[8,16,64,500]{3,2,1,0:T(8,128)(2,1)} %right_hbm.1, bf16[8,16,64,500]{3,2,1,0:T(8,128)(2,1)} %left_hbm.1), custom_call_target="tpu_custom_call" | custom-call | tf_op jit(solution)/shard_map/frames_to_commands/pallas_call | solution.py:359
  42.2 1.5 %copy.8 = f32[64,250]{1,0:T(8,128)} copy(f32[64,250]{1,0:T(8,128)} %frames_to_commands.1) | data formatting | bytes 128000
